TPU v7x, 32 devices: a whole 2x2x4 slice. The times are simulated.
32 devices in a mesh: dp: 16 (over z, y, core), mp: 2 (over x).
Axes of the slice: x: 2, y: 2, z: 4, core: 2. Of those that a mesh axis runs over, the one named last changes fastest.
Arguments:
- tokens: bfloat16 [2048, 2048], P('dp', 'mp'), may hold values from -32 to 32
- lengths: int32 [4], replicated, may hold values from 1 to 1536, 2048 in all
- keep_mask: int32 [2048], replicated, may hold values 0 or 1
- routes: int32 [2048, 8], P('dp'), may hold values from 0 to 63, all different within a row; in each aligned block of 128 rows (0 to 127, 128 to 255, ...) at most 32 rows name the same one
- attention_gain: float32 [2048], replicated, may hold values from 0.1 to 1.9
- mixture_gain: float32 [2048], P('mp'), may hold values from 0.1 to 1.9
- query_gain: float32 [128], replicated, may hold values from 0.5 to 8, as said below
- key_gain: float32 [128], replicated, may hold values from 0.5 to 8, as said below
- query_weight: bfloat16 [2048, 2048], P('dp', 'mp'), may hold values from -0.125 to 0.125
- key_weight: bfloat16 [2048, 2048], P('dp', 'mp'), may hold values from -0.125 to 0.125
- value_weight: bfloat16 [2048, 2048], P('dp', 'mp'), may hold values from -0.125 to 0.125
- output_weight: bfloat16 [2048, 2048], P('mp', 'dp'), may hold values from -0.1875 to 0.1875
- router_weight: float32 [2048, 64], P('mp'), may hold values from -0.125 to 0.125
- expert_gate: bfloat16 [16, 2048, 4096], P('dp', None, 'mp'), may hold values from -0.125 to 0.125
- expert_up: bfloat16 [16, 2048, 4096], P('dp', None, 'mp'), may hold values from -0.125 to 0.125
- expert_down: bfloat16 [16, 4096, 2048], P('dp', 'mp'), may hold values from -0.25 to 0.25
Outputs:
- layer_output: bfloat16 [2048, 2048], P('dp', 'mp')
Inputs may be any that keep to these rules, and one draw needn't show every extreme that they name: The lengths sum to 2048; exactly one is 1536. `routes`: each row names 8 different experts. Within each aligned block of 128 rows (the rows of one index of dp) no expert is named by more than 32 rows, a bound that some block reaches. `query_gain`: Positive. `key_gain`: Positive.
All inputs are finite; a program needn't handle non-finite values.
Results may differ from a plain program's by a relative error of at most 0.012.
The roundings to bfloat16 on the way count: a program that leaves them out, or rounds other values in their place, can miss the bound.
Values may be sent and summed in bfloat16 or wider, within the bound.
A program may use at most 128 MiB of HBM per device.

v0:
```python
import jax
import jax.numpy as jnp
from jax import lax
from jax.sharding import PartitionSpec as P

D = 2048
HEAD_DIM = 128
FF = 1024
EXPERTS = 64
TOPK = 8
CAP = 32
EPS = 1e-06
ROPE_BASE = 10000.0
NEG = -1e30


def rope_tables(position):
    halves = HEAD_DIM // 2
    exponent = jnp.arange(halves, dtype=jnp.float32) * (2.0 / HEAD_DIM)
    frequency = jnp.power(jnp.float32(ROPE_BASE), -exponent)
    angle = position.astype(jnp.float32)[:, None] * frequency[None, :]
    cos_table = jnp.cos(angle)
    sin_table = jnp.sin(angle)
    return (jnp.concatenate([cos_table, cos_table], 1), jnp.concatenate([sin_table, sin_table], 1))


def head_prep(projected, head_gain, cos_table, sin_table):
    row_count = projected.shape[0]
    per_head = projected.reshape(row_count, -1, HEAD_DIM)
    normed = (
        per_head * lax.rsqrt(jnp.mean(per_head * per_head, axis=2, keepdims=True) + EPS) * head_gain
    )
    halves = HEAD_DIM // 2
    rotated = jnp.concatenate([-normed[:, :, halves:], normed[:, :, :halves]], 2)
    turned = normed * cos_table[:, None, :] + rotated * sin_table[:, None, :]
    return turned.reshape(row_count, -1).astype(jnp.bfloat16)


def segment_info(lengths, global_row):
    request_end = jnp.cumsum(lengths)
    request_start = request_end - lengths
    segment = jnp.sum((request_end[None, :] <= global_row[:, None]).astype(jnp.int32), axis=1)
    chosen = segment[:, None] == jnp.arange(lengths.shape[0], dtype=jnp.int32)[None, :]
    begin = jnp.sum(jnp.where(chosen, request_start[None, :], 0), axis=1)
    return (segment, global_row - begin)


def gather_tokens(block):
    return lax.all_gather(block, "dp", axis=0, tiled=True)


def attention(queries, keys, values, query_seg, query_row, key_seg, key_row, keep_mask):
    scale = HEAD_DIM ** (-0.5)
    scores = (
        lax.dot_general(queries, keys, (((1,), (1,)), ((), ())), preferred_element_type=jnp.float32)
        * scale
    )
    visible = (query_seg[:, None] == key_seg[None, :]) & (
        (keep_mask[None, :] == 1) | (query_row[:, None] == key_row[None, :])
    )
    masked = jnp.where(visible, scores, NEG)
    top = jnp.max(masked, axis=1, keepdims=True)
    weights = jnp.where(visible, jnp.exp(masked - top), 0.0)
    totals = jnp.sum(weights, axis=1, keepdims=True)
    mixed = jnp.dot(weights.astype(jnp.bfloat16), values, preferred_element_type=jnp.float32)
    return (mixed / totals).astype(jnp.bfloat16)


def local(
    tokens,
    lengths,
    keep_mask,
    routes,
    attention_gain,
    mixture_gain,
    query_gain,
    key_gain,
    query_weight,
    key_weight,
    value_weight,
    output_weight,
    router_weight,
    expert_gate,
    expert_up,
    expert_down,
):
    tok_rows = tokens.shape[0]
    dp_count = lax.axis_size("dp")
    dp_index = lax.axis_index("dp")
    mp_index = lax.axis_index("mp")
    local_width = query_weight.shape[1]
    local_heads = local_width // HEAD_DIM
    share = dp_count // local_heads
    part = dp_index % share
    total_rows = tok_rows * dp_count
    weight_rows = query_weight.shape[0]
    packed = jnp.stack([query_weight, key_weight, value_weight]).reshape(
        3, weight_rows, local_heads, HEAD_DIM
    )
    packed = packed.transpose(2, 1, 0, 3).reshape(local_heads, weight_rows, 3 * HEAD_DIM)
    packed = jnp.repeat(packed, share, axis=0)
    head_weight = lax.all_to_all(packed, "dp", split_axis=0, concat_axis=0, tiled=True)
    head_weight = head_weight.reshape(dp_count * weight_rows, 3 * HEAD_DIM)
    full_tokens = lax.all_gather(tokens, "mp", axis=1, tiled=True)
    xfloat = full_tokens.astype(jnp.float32)
    normed_in = (
        xfloat * lax.rsqrt(jnp.mean(xfloat * xfloat, axis=1, keepdims=True) + EPS) * attention_gain
    ).astype(jnp.bfloat16)
    all_in = gather_tokens(normed_in)
    all_output_weight = lax.all_gather(output_weight, "dp", axis=1, tiled=True)
    key_row = jnp.arange(total_rows, dtype=jnp.int32)
    key_seg, key_pos = segment_info(lengths, key_row)
    cos_table, sin_table = rope_tables(key_pos)

    def own(array):
        split = array.reshape((local_heads, share, tok_rows) + array.shape[1:])
        taken = lax.dynamic_index_in_dim(split, part, 1, keepdims=False)
        return taken.reshape((local_heads * tok_rows,) + array.shape[1:])

    projected = jnp.dot(all_in, head_weight, preferred_element_type=jnp.float32)
    queries = head_prep(own(projected[:, :HEAD_DIM]), query_gain, own(cos_table), own(sin_table))
    keys = head_prep(projected[:, HEAD_DIM : 2 * HEAD_DIM], key_gain, cos_table, sin_table)
    values = projected[:, 2 * HEAD_DIM :].astype(jnp.bfloat16)
    attended = attention(
        queries, keys, values, own(key_seg), own(key_row), key_seg, key_row, keep_mask
    )
    groups = [[head * share + p for head in range(local_heads)] for p in range(share)]
    attended = lax.all_to_all(
        attended.reshape(local_heads, tok_rows, HEAD_DIM),
        "dp",
        split_axis=0,
        concat_axis=0,
        tiled=True,
        axis_index_groups=groups,
    )
    attended = attended.transpose(1, 0, 2).reshape(tok_rows, local_width)
    partial_out = jnp.dot(attended, all_output_weight, preferred_element_type=jnp.float32)
    summed_out = lax.psum_scatter(partial_out, "mp", scatter_dimension=1, tiled=True)
    residual = (tokens.astype(jnp.float32) + summed_out).astype(jnp.bfloat16)
    hfloat = residual.astype(jnp.float32)
    scaled = hfloat * mixture_gain
    partial_logits = jnp.dot(scaled, router_weight, precision=lax.Precision.HIGHEST)
    square_sum, logit_sum = lax.psum((jnp.sum(hfloat * hfloat, axis=1), partial_logits), "mp")
    inverse = lax.rsqrt(square_sum / D + EPS)[:, None]
    mixed_in = (scaled * inverse).astype(jnp.bfloat16)
    logits = logit_sum * inverse
    experts = jnp.arange(EXPERTS, dtype=jnp.int32)
    named = jnp.any(routes[None, :, :] == experts[:, None, None], axis=2)
    named_float = named.astype(jnp.float32)
    sigmoid_vals = jax.nn.sigmoid(logits).T * named_float
    route_weight = sigmoid_vals / jnp.sum(sigmoid_vals, axis=0, keepdims=True)
    ids = jnp.arange(tok_rows, dtype=jnp.int32)
    earlier = (ids[:, None] < ids[None, :]).astype(jnp.bfloat16)
    before = jnp.dot(named.astype(jnp.bfloat16), earlier, preferred_element_type=jnp.float32)
    place = jnp.where(named, before.astype(jnp.int32), -1)
    exp_local = EXPERTS // dp_count
    gate_local = expert_gate[0]
    up_local = expert_up[0]
    down_local = expert_down[0]
    unit_count = gate_local.shape[1]
    held = max(1, unit_count // FF)
    units = unit_count // held
    first_expert = mp_index * unit_count // FF

    def mine(table):
        split = table.reshape(dp_count, exp_local, tok_rows)
        return lax.dynamic_slice_in_dim(split, first_expert, held, 1)

    slots = jnp.arange(CAP, dtype=jnp.int32)
    chosen = mine(place)[:, :, None, :] == slots[None, None, :, None]
    select = chosen.astype(jnp.bfloat16).reshape(dp_count * held * CAP, tok_rows)
    full_in = lax.all_gather(mixed_in, "mp", axis=1, tiled=True)
    sending = jnp.dot(select, full_in, preferred_element_type=jnp.float32).astype(jnp.bfloat16)
    rows_in = lax.all_to_all(
        sending.reshape(dp_count, held, CAP, D), "dp", split_axis=0, concat_axis=0, tiled=True
    )
    outs = []
    for index in range(held):
        rows = rows_in[:, index].reshape(dp_count * CAP, D)
        low, high = (index * units, (index + 1) * units)
        gate_val = jnp.dot(rows, gate_local[:, low:high], preferred_element_type=jnp.float32)
        up_val = jnp.dot(rows, up_local[:, low:high], preferred_element_type=jnp.float32)
        hidden = (jax.nn.silu(gate_val) * up_val).astype(jnp.bfloat16)
        out = jnp.dot(hidden, down_local[low:high], preferred_element_type=jnp.float32)
        outs.append(out.astype(jnp.bfloat16).reshape(dp_count, CAP, D))
    returned = lax.all_to_all(
        jnp.stack(outs, axis=1), "dp", split_axis=0, concat_axis=0, tiled=True
    ).reshape(dp_count * held * CAP, D)
    spread = jnp.where(chosen, mine(route_weight)[:, :, None, :], 0.0)
    spread = spread.reshape(dp_count * held * CAP, tok_rows)
    spread_high = spread.astype(jnp.bfloat16)
    spread_mid = (spread - spread_high.astype(jnp.float32)).astype(jnp.bfloat16)
    contract = (((0,), (0,)), ((), ()))
    mixture = lax.dot_general(
        spread_high, returned, contract, preferred_element_type=jnp.float32
    ) + lax.dot_general(spread_mid, returned, contract, preferred_element_type=jnp.float32)
    mixture = lax.psum_scatter(mixture, "mp", scatter_dimension=1, tiled=True)
    return (hfloat + mixture).astype(jnp.bfloat16)


def solution(mesh):
    return jax.shard_map(
        local,
        mesh=mesh,
        in_specs=(
            P("dp", "mp"),
            P(),
            P(),
            P("dp", None),
            P(),
            P("mp"),
            P(),
            P(),
            P("dp", "mp"),
            P("dp", "mp"),
            P("dp", "mp"),
            P("mp", "dp"),
            P("mp", None),
            P("dp", None, "mp"),
            P("dp", None, "mp"),
            P("dp", "mp", None),
        ),
        out_specs=P("dp", "mp"),
        check_vma=False,
    )
```

profile of v0, /device:TPU:0, one launch (start us, length us, event | category | flops | bytes accessed | tf_op | source)
XLA Modules:
  0.0 488.3 jit_solution(367880626133548728)
XLA Ops:
  6.5 10.3 %all_gather.12 = bf16[128,2048]{1,0:T(8,128)(2,1)S(1)} all-gather(bf16[128,1024]{1,0:T(8,128)(2,1)} %param.16), channel_id=1, replica_groups=mesh['dp'=16,'mp'=2] {'mp'}, dimensions={1}, use_global_device_ids=true | all-gather | bytes 786432 | tf_op jit(solution)/shard_map/all_gather | solution.py:104
  17.0 1.7 fusion.35
  18.7 1.1 copy.39
  19.9 1.1 copy.40
  21.0 1.1 copy.41
  22.2 0.4 copy.42
  22.6 1.4 broadcast_in_dim.32
  24.0 6.2 %all-to-all-start = ((bf16[16,128,384]{2,1,0:T(8,128)(2,1)}), bf16[16,128,384]{2,1,0:T(8,128)(2,1)}, u32[]{:S(2)}, u32[]{:S(2)}) async-start(bf16[16,128,384]{2,1,0:T(8,128)(2,1)} %bitcast.10), calls=%async_computation | async-start | bytes 3145728 | tf_op jit(solution)/shard_map/all_to_all | solution.py:102
  30.3 0.7 all-gather.5.cloned.1.call-update
  31.5 3.7 multiply_cosine_fusion
  35.2 3.3 multiply_sine_fusion.1
  38.4 39.1 %all-to-all-done = bf16[16,128,384]{2,1,0:T(8,128)(2,1)} async-done(((bf16[16,128,384]{2,1,0:T(8,128)(2,1)}), bf16[16,128,384]{2,1,0:T(8,128)(2,1)}, u32[]{:S(2)}, u32[]{:S(2)}) %all-to-all-start) | async-done | bytes 1572896 | tf_op jit(solution)/shard_map/all_to_all | solution.py:102
  77.6 43.2 %all-gather.3.cloned.1.call-done = bf16[2048,2048]{1,0:T(8,128)(2,1)} async-done(((bf16[128,2048]{1,0:T(8,128)(2,1)}), bf16[2048,2048]{1,0:T(8,128)(2,1)}) %all-gather.3.cloned.1.call-update) | async-done | bytes 8388624 | tf_op jit(solution)/shard_map/all_gather | solution.py:49
  120.7 6.4 %fusion.88 = f32[2048,384]{0,1:T(8,128)S(1)} fusion(bf16[2048,2048]{1,0:T(8,128)(2,1)} %all-gather.3.cloned.1.call-done, bf16[2048,384]{1,0:T(8,128)(2,1)} %bitcast.11), kind=kOutput, calls=%fused_computation.130 | convolution fusion | flops 3221225472 | bytes 13107200 | tf_op jit(solution)/shard_map/dot_general | solution.py:120
  127.2 1.5 copy-done.3
  128.8 1.2 fusion.48
  130.0 1.9 reshape.358
  131.9 1.7 constant_dynamic-slice_fusion.2
  133.6 0.4 copy.50
  134.6 0.6 fusion.60
  135.4 1.0 copy-done.4
  136.6 3.4 fusion.2
  140.1 5.0 %fusion.3 = f32[1024]{0:T(1024)S(1)} fusion(f32[1024,2048]{1,0:T(8,128)S(1)} %get-tuple-element.24, f32[1024]{0:T(1024)S(1)} %get-tuple-element.23, s32[1024]{0:T(1024)S(1)} %bitcast.112, pred[2048]{0:T(1024)(128)(4,1)S(1)} %broadcast_compare_fusion, s32[2048]{0:T(1024)S(1)} %convert_reduce_fusion, s32[1024]{0:T(1024)S(1)} %bitcast.115), kind=kLoop, calls=%fused_computation.6 | loop fusion | flops 18873344 | bytes 8415232 | tf_op jit(solution)/shard_map/reduce_sum | solution.py:64
  145.0 3.9 fusion.45
  148.9 0.9 copy.45
  149.8 3.5 all-to-all-start.1
  153.4 24.8 %all-gather.5.cloned.1.call-done = bf16[1024,2048]{1,0:T(8,128)(2,1)} async-done(((bf16[1024,128]{1,0:T(8,128)(2,1)}), bf16[1024,2048]{1,0:T(8,128)(2,1)}) %all-gather.5.cloned.1.call-update) | async-done | bytes 4194320 | tf_op jit(solution)/shard_map/all_gather | solution.py:110
  178.2 3.9 fusion.89
  182.7 20.2 %reduce-scatter.3.cloned.1.call-done = f32[128,1024]{1,0:T(8,128)} async-done(((f32[128,2048]{1,0:T(8,128)}), f32[128,1024]{1,0:T(8,128)}) %reduce-scatter.3.cloned.1.call-update) | async-done | bytes 524304 | tf_op jit(solution)/shard_map/reduce_scatter | solution.py:138
  203.0 1.2 fusion.53
  204.2 0.7 fusion.50
  204.8 7.3 %all-reduce = (f32[128]{0:T(128)S(1)}, f32[128,64]{0,1:T(8,128)S(1)}) all-reduce(f32[128]{0:T(128)S(1)} %get-tuple-element.7, f32[128,64]{0,1:T(8,128)S(1)} %fusion.50), channel_id=1, replica_groups=mesh['dp'=16,'mp'=2] {'mp'}, use_global_device_ids=true, to_apply=%region_12.13 | all-reduce | flops 8320 | bytes 66560 | tf_op jit(solution)/shard_map/psum | solution.py:143
  212.2 7.0 %all_gather.15 = bf16[128,2048]{1,0:T(8,128)(2,1)S(1)} all-gather(bf16[128,1024]{1,0:T(8,128)(2,1)S(1)} %fusion.51), channel_id=1, replica_groups=mesh['dp'=16,'mp'=2] {'mp'}, dimensions={1}, use_global_device_ids=true | all-gather | bytes 786432 | tf_op jit(solution)/shard_map/all_gather | solution.py:172
  219.3 1.2 convolution_convert_fusion
  220.5 98.4 %all_to_all.20 = bf16[16,2,32,2048]{3,2,1,0:T(8,128)(2,1)S(1)} all-to-all(bf16[16,2,32,2048]{3,2,1,0:T(8,128)(2,1)S(1)} %bitcast.92), channel_id=1, replica_groups=mesh['dp'=16,'mp'=2] {'dp'}, dimensions={0} | all-to-all | bytes 8388608 | tf_op jit(solution)/shard_map/all_to_all | solution.py:174
  319.0 0.4 fusion.87
  319.4 2.5 slice-done.1
  321.9 3.7 fusion.11
  325.6 3.7 fusion.7
  329.3 10.5 %fusion.21 = bf16[512,2048]{1,0:T(8,128)(2,1)} fusion(bf16[1,2048,2048]{2,1,0:T(8,128)(2,1)} %param.31, f32[512,1024]{1,0:T(8,128)} %fusion.11, bf16[512,2048]{1,0:T(8,128)(2,1)} %bitcast.99, bf16[2048,2048]{1,0:T(8,128)(2,1)} %bitcast.123), kind=kOutput, calls=%fused_computation.25 | convolution fusion | flops 4299161600 | bytes 14680064 | tf_op jit(solution)/shard_map/dot_general | solution.py:184
  339.9 9.9 %fusion.24 = bf16[512,2048]{1,0:T(8,128)(2,1)} fusion(bf16[1,2048,2048]{2,1,0:T(8,128)(2,1)} %param.31, f32[512,1024]{1,0:T(8,128)} %fusion.7, bf16[512,2048]{1,0:T(8,128)(2,1)S(1)} %bitcast.97, bf16[2048,2048]{1,0:T(8,128)(2,1)} %bitcast.124), kind=kOutput, calls=%fused_computation.26 | convolution fusion | flops 4299161600 | bytes 14680064 | tf_op jit(solution)/shard_map/dot_general | solution.py:184
  349.8 4.6 pad_maximum_fusion
  354.4 5.3 %all-to-all-start.3 = ((bf16[16,2,32,2048]{3,2,1,0:T(8,128)(2,1)}), bf16[16,2,32,2048]{3,2,1,0:T(8,128)(2,1)}, u32[]{:S(2)}, u32[]{:S(2)}) async-start(bf16[16,2,32,2048]{3,2,1,0:T(8,128)(2,1)} %pad_maximum_fusion), calls=%async_computation.4 | async-start | bytes 8388608 | tf_op jit(solution)/shard_map/all_to_all | solution.py:186
  359.9 77.5 %all-to-all-done.3 = bf16[16,2,32,2048]{3,2,1,0:T(8,128)(2,1)} async-done(((bf16[16,2,32,2048]{3,2,1,0:T(8,128)(2,1)}), bf16[16,2,32,2048]{3,2,1,0:T(8,128)(2,1)}, u32[]{:S(2)}, u32[]{:S(2)}) %all-to-all-start.3) | async-done | bytes 4194336 | tf_op jit(solution)/shard_map/all_to_all | solution.py:186
  437.4 3.0 convolution_bitcast_fusion
  440.4 3.9 fusion.27
  444.3 35.4 %reduce-scatter.5.cloned.1.call-done = f32[128,1024]{1,0:T(8,128)} async-done(((f32[128,2048]{1,0:T(8,128)}), f32[128,1024]{1,0:T(8,128)}) %reduce-scatter.5.cloned.1.call-update) | async-done | bytes 524304 | tf_op jit(solution)/shard_map/reduce_scatter | solution.py:197
  479.7 1.8 fusion.54
  (72 shorter events, 2.7 us)
Async XLA Ops:
  6.5 197.6 %copy-start = (f32[1024,64]{0,1:T(8,128)S(1)}, f32[1024,64]{0,1:T(8,128)}, u32[]{:S(2)}) copy-start(f32[1024,64]{0,1:T(8,128)} %param.28) | copy-start | bytes 786436
  6.5 114.2 %all-gather.3.cloned.1.call-start = ((), (), s32[]{:S(2)}) async-start(), calls=%async_computation.6 | async-start | bytes 8912896 | tf_op jit(solution)/shard_map/all_gather | solution.py:49
  22.1 8.8 %copy-start.14 = (s32[4]{0:T(128)S(1)}, s32[4]{0:T(128)}, u32[]{:S(2)}) copy-start(s32[4]{0:T(128)} %param.17) | copy-start | bytes 52
  22.1 9.3 %copy-start.10 = (s32[2048]{0:T(1024)S(1)}, s32[2048]{0:T(1024)}, u32[]{:S(2)}) copy-start(s32[2048]{0:T(1024)} %param.18) | copy-start | bytes 24580
  24.0 53.6 %all-to-all-start = ((bf16[16,128,384]{2,1,0:T(8,128)(2,1)}), bf16[16,128,384]{2,1,0:T(8,128)(2,1)}, u32[]{:S(2)}, u32[]{:S(2)}) async-start(bf16[16,128,384]{2,1,0:T(8,128)(2,1)} %bitcast.10), calls=%async_computation | async-start | bytes 3145728 | tf_op jit(solution)/shard_map/all_to_all | solution.py:102
  30.2 148.0 %all-gather.5.cloned.1.call-start = ((), (), s32[]{:S(2)}) async-start(), calls=%async_computation.7 | async-start | bytes 4456448 | tf_op jit(solution)/shard_map/all_gather | solution.py:110
  120.7 8.0 %copy-start.13 = (f32[128]{0:T(128)S(1)}, f32[128]{0:T(128)}, u32[]{:S(2)}) copy-start(f32[128]{0:T(128)} %param.23) | copy-start | bytes 1540
  127.1 1.7 copy-start.3
  128.8 5.4 %copy-start.12 = (f32[128]{0:T(128)S(1)}, f32[128]{0:T(128)}, u32[]{:S(2)}) copy-start(f32[128]{0:T(128)} %param.22) | copy-start | bytes 1540
  134.0 1.3 copy-start.2
  134.4 2.0 copy-start.4
  134.4 2.1 copy-start.7
  134.4 2.2 copy-start.8
  148.9 33.4 %copy-start.11 = (s32[128,8]{0,1:T(8,128)S(1)}, s32[128,8]{0,1:T(8,128)}, u32[]{:S(2)}) copy-start(s32[128,8]{0,1:T(8,128)} %param.19) | copy-start | bytes 12292
  148.9 54.0 %copy-start.6 = (bf16[128,1024]{1,0:T(8,128)(2,1)S(1)}, bf16[128,1024]{1,0:T(8,128)(2,1)}, u32[]{:S(2)}) copy-start(bf16[128,1024]{1,0:T(8,128)(2,1)} %param.16) | copy-start | bytes 786436
  149.8 54.4 %copy-start.9 = (f32[1024]{0:T(1024)S(1)}, f32[1024]{0:T(1024)}, u32[]{:S(2)}) copy-start(f32[1024]{0:T(1024)} %param.21) | copy-start | bytes 12292
  149.8 28.4 %all-to-all-start.1 = ((bf16[8,128,128]{1,2,0:T(8,128)(2,1)}), bf16[8,128,128]{1,2,0:T(8,128)(2,1)S(1)}, u32[]{:S(2)}, u32[]{:S(2)}) async-start(bf16[8,128,128]{1,2,0:T(8,128)(2,1)} %copy.45), calls=%async_computation.1 | async-start | bytes 524288 | tf_op jit(solution)/shard_map/all_to_all | solution.py:128
  153.3 49.6 %reduce-scatter.3.cloned.1.call-start = ((), (), s32[]{:S(2)}) async-start(), calls=%async_computation.8 | async-start | bytes 1572864 | tf_op jit(solution)/shard_map/reduce_scatter | solution.py:138
  220.5 98.9 %slice-start = ((s8[8388608]{0:T(1024)(128)(4,1)}), s8[4194304]{0:T(1024)(128)(4,1)S(1)}, s32[]{:S(2)}) async-start(s8[8388608]{0:T(1024)(128)(4,1)} %bitcast.119), calls=%async_computation.10 | async-start | bytes 8388608
  318.9 2.9 slice-start.1
  319.4 6.2 %copy-start.5 = (bf16[16,1,32,2048]{3,2,1,0:T(8,128)(2,1)}, bf16[16,1,32,2048]{3,2,1,0:T(8,128)(2,1)S(1)}, u32[]{:S(2)}) copy-start(bf16[16,1,32,2048]{3,2,1,0:T(8,128)(2,1)S(1)} %get-tuple-element.9) | copy-start | bytes 6291460
  354.4 83.0 %all-to-all-start.3 = ((bf16[16,2,32,2048]{3,2,1,0:T(8,128)(2,1)}), bf16[16,2,32,2048]{3,2,1,0:T(8,128)(2,1)}, u32[]{:S(2)}, u32[]{:S(2)}) async-start(bf16[16,2,32,2048]{3,2,1,0:T(8,128)(2,1)} %pad_maximum_fusion), calls=%async_computation.4 | async-start | bytes 8388608 | tf_op jit(solution)/shard_map/all_to_all | solution.py:186
  359.7 120.0 %reduce-scatter.5.cloned.1.call-start = ((), (), s32[]{:S(2)}) async-start(), calls=%async_computation.9 | async-start | bytes 1572864 | tf_op jit(solution)/shard_map/reduce_scatter | solution.py:197
  437.4 44.1 %copy-start.1 = (f32[1024,64]{0,1:T(8,128)S(1)}, f32[1024,64]{0,1:T(8,128)}, u32[]{:S(2)}) copy-start(f32[1024,64]{0,1:T(8,128)} %param.28) | copy-start | bytes 786436
Sparse Core Ops, SparseCore 0:
  18.9 101.8 all-gather.2
  122.9 55.2 all-gather.4
  182.3 20.6 reduce-scatter.2
  444.4 35.2 reduce-scatter.4
where the time goes:
time: 494 us; the launch traced here: 488 us
  waiting for transfers between devices  241 us (49%)
  blocking collectives  123 us (25%)
  matrix products  54.4 us (11%)
  other arithmetic  25 us (5%)
  local copies, waits for them, and re-layouts  15.8 us (3%)
  starting transfers between devices  15.2 us (3%)
  between operations  13.8 us (3%)
    all_to_all x1, blocking collectives, local(): lax.all_to_all(sending.reshape(dp_count, held, CAP, D), 'dp', split_axis=...  98.4 us
    all_to_all x1, waiting for transfers between devices, local(): lax.all_to_all(jnp.stack(outs, axis=1), 'dp', split_axis=0, concat_axis=0...  77.5 us
    all_gather x1, waiting for transfers between devices, gather_tokens(): return lax.all_gather(block, 'dp', axis=0, tiled=True)  43.2 us
    all_to_all x1, waiting for transfers between devices, local(): lax.all_to_all(packed, 'dp', split_axis=0, concat_axis=0, tiled=True)  39.1 us
    reduce_scatter x1, waiting for transfers between devices, local(): mixture = lax.psum_scatter(mixture, 'mp', scatter_dimension=1, tiled=True)  35.4 us
    all_gather x1, waiting for transfers between devices, local(): all_output_weight = lax.all_gather(output_weight, 'dp', axis=1, tiled=True)  24.8 us
    dot_general x2, matrix products, local(): jnp.dot(hidden, down_local[low:high], preferred_element_type=jnp.float32)  20.5 us
    reduce_scatter x1, waiting for transfers between devices, local(): lax.psum_scatter(partial_out, 'mp', scatter_dimension=1, tiled=True)  20.2 us
  transfers between devices with their start and end apart: 7, of which 6 were waited for; matrix products, arithmetic and copies ran while one was open for 8% of the time, Pallas kernels for 0%

commit v1 on v0

--- a/solution.py
+++ b/solution.py
@@ -107,7 +107,12 @@
         xfloat * lax.rsqrt(jnp.mean(xfloat * xfloat, axis=1, keepdims=True) + EPS) * attention_gain
     ).astype(jnp.bfloat16)
     all_in = gather_tokens(normed_in)
-    all_output_weight = lax.all_gather(output_weight, "dp", axis=1, tiled=True)
+    ring = [output_weight]
+    for hop in range(15):
+        ring.append(lax.ppermute(ring[-1], "dp", [(dev, (dev + 1) % 16) for dev in range(16)]))
+    all_output_weight = jnp.roll(
+        jnp.concatenate(ring[::-1], axis=1), (lax.axis_index("dp") + 1) * ring[0].shape[1], axis=1
+    )
     key_row = jnp.arange(total_rows, dtype=jnp.int32)
     key_seg, key_pos = segment_info(lengths, key_row)
     cos_table, sin_table = rope_tables(key_pos)

time: 494 us -> 600 us (1.21)
  waiting for transfers between devices: 241 us -> 299 us
  local copies, waits for them, and re-layouts: 15.8 us -> 56.9 us
    ppermute x0 -> x15, waiting for transfers between devices: none -> 163 us  [local(): lax.ppermute(ring[-1], 'dp', [(dev, (dev + 1) % 16) for dev in range(16)])]
    all_gather x1, waiting for transfers between devices: 43.2 us -> 0.01 us  [gather_tokens(): return lax.all_gather(block, 'dp', axis=0, tiled=True)]
    unnamed x38 -> x109, local copies, waits for them, and re-layouts: 9.08 us -> 49.4 us
    all_to_all x1, waiting for transfers between devices: 39.1 us -> 0.01 us  [local(): lax.all_to_all(packed, 'dp', split_axis=0, concat_axis=0, tiled=True)]
    all_gather x1 -> x0, waiting for transfers between devices: 24.8 us -> none  [local(): all_output_weight = lax.all_gather(output_weight, 'dp', axis=1, tiled=True)]
  transfers between devices with their start and end apart: 7 -> 21, of which waited for: 6 -> 18; matrix products, arithmetic and copies ran while one was open for 8% -> 9% of each run, Pallas kernels for 0% -> 0%
where the time goes in v1:
time: 600 us; the launch traced here: 592 us
  waiting for transfers between devices  299 us (50%)
  blocking collectives  123 us (20%)
  matrix products  58.5 us (10%)
  local copies, waits for them, and re-layouts  56.9 us (9%)
  other arithmetic  25 us (4%)
  starting transfers between devices  15.1 us (3%)
  between operations  14 us (2%)
    ppermute x15, waiting for transfers between devices, local(): lax.ppermute(ring[-1], 'dp', [(dev, (dev + 1) % 16) for dev in range(16)])  163 us
    all_to_all x1, blocking collectives, local(): lax.all_to_all(sending.reshape(dp_count, held, CAP, D), 'dp', split_axis=...  98.4 us
    all_to_all x1, waiting for transfers between devices, local(): lax.all_to_all(jnp.stack(outs, axis=1), 'dp', split_axis=0, concat_axis=0...  77.5 us
    unnamed x109, local copies, waits for them, and re-layouts  49.4 us
    reduce_scatter x1, waiting for transfers between devices, local(): mixture = lax.psum_scatter(mixture, 'mp', scatter_dimension=1, tiled=True)  35.4 us
    dot_general x2, matrix products, local(): jnp.dot(hidden, down_local[low:high], preferred_element_type=jnp.float32)  20.6 us
    reduce_scatter x1, waiting for transfers between devices, local(): lax.psum_scatter(partial_out, 'mp', scatter_dimension=1, tiled=True)  18.1 us
  transfers between devices with their start and end apart: 21, of which 18 were waited for; matrix products, arithmetic and copies ran while one was open for 9% of the time, Pallas kernels for 0%

profile of v1, /device:TPU:0, one launch (start us, length us, event | category | flops | bytes accessed | tf_op | source)
XLA Modules:
  0.0 591.7 jit_solution(8289419139772092362)
XLA Ops:
  6.5 10.3 %all_gather.9 = bf16[128,2048]{1,0:T(8,128)(2,1)S(1)} all-gather(bf16[128,1024]{1,0:T(8,128)(2,1)} %param.16), channel_id=1, replica_groups=mesh['dp'=16,'mp'=2] {'mp'}, dimensions={1}, use_global_device_ids=true | all-gather | bytes 786432 | tf_op jit(solution)/shard_map/all_gather | solution.py:104
  18.8 8.7 %collective-permute-done = bf16[1024,128]{1,0:T(8,128)(2,1)S(1)} collective-permute-done((bf16[1024,128]{1,0:T(8,128)(2,1)}, bf16[1024,128]{1,0:T(8,128)(2,1)S(1)}, u32[]{:S(2)}, u32[]{:S(2)}) %collective-permute-start) | collective-permute-done | bytes 262176 | tf_op jit(solution)/shard_map/ppermute | solution.py:112
  27.5 12.2 %collective-permute-done.1 = bf16[1024,128]{1,0:T(8,128)(2,1)S(1)} collective-permute-done((bf16[1024,128]{1,0:T(8,128)(2,1)S(1)}, bf16[1024,128]{1,0:T(8,128)(2,1)S(1)}, u32[]{:S(2)}, u32[]{:S(2)}) %collective-permute-start.1) | collective-permute-done | bytes 262176 | tf_op jit(solution)/shard_map/ppermute | solution.py:112
  39.7 14.1 %collective-permute-done.2 = bf16[1024,128]{1,0:T(8,128)(2,1)S(1)} collective-permute-done((bf16[1024,128]{1,0:T(8,128)(2,1)S(1)}, bf16[1024,128]{1,0:T(8,128)(2,1)S(1)}, u32[]{:S(2)}, u32[]{:S(2)}) %collective-permute-start.2) | collective-permute-done | bytes 262176 | tf_op jit(solution)/shard_map/ppermute | solution.py:112
  53.8 8.6 %collective-permute-done.3 = bf16[1024,128]{1,0:T(8,128)(2,1)S(1)} collective-permute-done((bf16[1024,128]{1,0:T(8,128)(2,1)S(1)}, bf16[1024,128]{1,0:T(8,128)(2,1)S(1)}, u32[]{:S(2)}, u32[]{:S(2)}) %collective-permute-start.3) | collective-permute-done | bytes 262176 | tf_op jit(solution)/shard_map/ppermute | solution.py:112
  63.1 14.1 %collective-permute-done.4 = bf16[1024,128]{1,0:T(8,128)(2,1)S(1)} collective-permute-done((bf16[1024,128]{1,0:T(8,128)(2,1)S(1)}, bf16[1024,128]{1,0:T(8,128)(2,1)S(1)}, u32[]{:S(2)}, u32[]{:S(2)}) %collective-permute-start.4) | collective-permute-done | bytes 262176 | tf_op jit(solution)/shard_map/ppermute | solution.py:112
  77.9 14.1 %collective-permute-done.5 = bf16[1024,128]{1,0:T(8,128)(2,1)S(1)} collective-permute-done((bf16[1024,128]{1,0:T(8,128)(2,1)S(1)}, bf16[1024,128]{1,0:T(8,128)(2,1)S(1)}, u32[]{:S(2)}, u32[]{:S(2)}) %collective-permute-start.5) | collective-permute-done | bytes 262176 | tf_op jit(solution)/shard_map/ppermute | solution.py:112
  92.7 13.3 %collective-permute-done.6 = bf16[1024,128]{1,0:T(8,128)(2,1)S(1)} collective-permute-done((bf16[1024,128]{1,0:T(8,128)(2,1)S(1)}, bf16[1024,128]{1,0:T(8,128)(2,1)S(1)}, u32[]{:S(2)}, u32[]{:S(2)}) %collective-permute-start.6) | collective-permute-done | bytes 262176 | tf_op jit(solution)/shard_map/ppermute | solution.py:112
  106.7 8.5 %collective-permute-done.7 = bf16[1024,128]{1,0:T(8,128)(2,1)S(1)} collective-permute-done((bf16[1024,128]{1,0:T(8,128)(2,1)S(1)}, bf16[1024,128]{1,0:T(8,128)(2,1)S(1)}, u32[]{:S(2)}, u32[]{:S(2)}) %collective-permute-start.7) | collective-permute-done | bytes 262176 | tf_op jit(solution)/shard_map/ppermute | solution.py:112
  120.6 5.8 all-to-all-start
  127.1 33.5 %collective-permute-done.9 = bf16[1024,128]{1,0:T(8,128)(2,1)S(1)} collective-permute-done((bf16[1024,128]{1,0:T(8,128)(2,1)S(1)}, bf16[1024,128]{1,0:T(8,128)(2,1)S(1)}, u32[]{:S(2)}, u32[]{:S(2)}) %collective-permute-start.9) | collective-permute-done | bytes 262176 | tf_op jit(solution)/shard_map/ppermute | solution.py:112
  161.3 8.6 %collective-permute-done.10 = bf16[1024,128]{1,0:T(8,128)(2,1)S(1)} collective-permute-done((bf16[1024,128]{1,0:T(8,128)(2,1)S(1)}, bf16[1024,128]{1,0:T(8,128)(2,1)S(1)}, u32[]{:S(2)}, u32[]{:S(2)}) %collective-permute-start.10) | collective-permute-done | bytes 262176 | tf_op jit(solution)/shard_map/ppermute | solution.py:112
  170.6 2.8 multiply_sine_fusion.1
  173.4 5.7 collective-permute-done.11
  179.1 8.4 %collective-permute-done.12 = bf16[1024,128]{1,0:T(8,128)(2,1)S(1)} collective-permute-done((bf16[1024,128]{1,0:T(8,128)(2,1)S(1)}, bf16[1024,128]{1,0:T(8,128)(2,1)S(1)}, u32[]{:S(2)}, u32[]{:S(2)}) %collective-permute-start.12) | collective-permute-done | bytes 262176 | tf_op jit(solution)/shard_map/ppermute | solution.py:112
  187.6 8.5 %collective-permute-done.13 = bf16[1024,128]{1,0:T(8,128)(2,1)} collective-permute-done((bf16[1024,128]{1,0:T(8,128)(2,1)S(1)}, bf16[1024,128]{1,0:T(8,128)(2,1)}, u32[]{:S(2)}, u32[]{:S(2)}) %collective-permute-start.13) | collective-permute-done | bytes 262176 | tf_op jit(solution)/shard_map/ppermute | solution.py:112
  196.3 3.7 multiply_cosine_fusion
  200.0 5.0 collective-permute-done.14
  205.7 1.7 constant_dynamic-update-slice_fusion.30
  209.1 1.7 constant_dynamic-update-slice_fusion.28
  214.2 1.7 constant_dynamic-update-slice_fusion.25
  217.7 1.7 constant_dynamic-update-slice_fusion.23
  222.8 1.7 constant_dynamic-update-slice_fusion.20
  239.6 1.7 constant_dynamic-update-slice_fusion.4
  241.3 6.8 %fusion.91 = f32[2048,384]{0,1:T(8,128)S(1)} fusion(bf16[2048,2048]{1,0:T(8,128)(2,1)} %all-gather.2.cloned.1.call-done, bf16[2048,384]{1,0:T(8,128)(2,1)} %bitcast.11), kind=kOutput, calls=%fused_computation.165 | convolution fusion | flops 3221225472 | bytes 13107200 | tf_op jit(solution)/shard_map/dot_general | solution.py:125
  250.2 1.9 reshape.358
  255.4 5.6 fusion.2
  261.0 5.0 fusion.3
  266.0 5.2 fusion.47
  272.1 3.4 all-to-all-start.1
  278.7 5.0 all-to-all-done.1
  283.7 3.9 fusion.19
  288.2 18.1 %reduce-scatter.3.cloned.1.call-done = f32[128,1024]{1,0:T(8,128)} async-done(((f32[128,2048]{1,0:T(8,128)}), f32[128,1024]{1,0:T(8,128)}) %reduce-scatter.3.cloned.1.call-update) | async-done | bytes 524304 | tf_op jit(solution)/shard_map/reduce_scatter | solution.py:143
  308.2 7.3 %all-reduce = (f32[128]{0:T(128)S(1)}, f32[128,64]{0,1:T(8,128)S(1)}) all-reduce(f32[128]{0:T(128)S(1)} %get-tuple-element.7, f32[128,64]{0,1:T(8,128)S(1)} %fusion.52), channel_id=1, replica_groups=mesh['dp'=16,'mp'=2] {'mp'}, use_global_device_ids=true, to_apply=%region_12.13 | all-reduce | flops 8320 | bytes 66560 | tf_op jit(solution)/shard_map/psum | solution.py:148
  315.6 7.0 %all_gather.11 = bf16[128,2048]{1,0:T(8,128)(2,1)S(1)} all-gather(bf16[128,1024]{1,0:T(8,128)(2,1)S(1)} %fusion.53), channel_id=1, replica_groups=mesh['dp'=16,'mp'=2] {'mp'}, dimensions={1}, use_global_device_ids=true | all-gather | bytes 786432 | tf_op jit(solution)/shard_map/all_gather | solution.py:177
  323.9 98.4 %all_to_all.20 = bf16[16,2,32,2048]{3,2,1,0:T(8,128)(2,1)S(1)} all-to-all(bf16[16,2,32,2048]{3,2,1,0:T(8,128)(2,1)S(1)} %bitcast.91), channel_id=1, replica_groups=mesh['dp'=16,'mp'=2] {'dp'}, dimensions={0} | all-to-all | bytes 8388608 | tf_op jit(solution)/shard_map/all_to_all | solution.py:179
  422.7 2.5 slice-done.1
  425.2 3.7 fusion.7
  428.9 3.8 fusion.11
  432.7 10.6 %fusion.26 = bf16[512,2048]{1,0:T(8,128)(2,1)} fusion(bf16[1,2048,2048]{2,1,0:T(8,128)(2,1)} %param.31, f32[512,1024]{1,0:T(8,128)} %fusion.7, bf16[512,2048]{1,0:T(8,128)(2,1)} %bitcast.98, bf16[2048,2048]{1,0:T(8,128)(2,1)} %bitcast.122), kind=kOutput, calls=%fused_computation.28 | convolution fusion | flops 4299161600 | bytes 14680064 | tf_op jit(solution)/shard_map/dot_general | solution.py:189
  443.3 10.0 %fusion.23 = bf16[512,2048]{1,0:T(8,128)(2,1)} fusion(bf16[1,2048,2048]{2,1,0:T(8,128)(2,1)} %param.31, f32[512,1024]{1,0:T(8,128)} %fusion.11, bf16[512,2048]{1,0:T(8,128)(2,1)S(1)} %bitcast.96, bf16[2048,2048]{1,0:T(8,128)(2,1)} %bitcast.123), kind=kOutput, calls=%fused_computation.27 | convolution fusion | flops 4299161600 | bytes 14680064 | tf_op jit(solution)/shard_map/dot_general | solution.py:189
  453.3 4.6 pad_maximum_fusion
  457.8 5.3 all-to-all-start.3
  463.3 77.5 %all-to-all-done.3 = bf16[16,2,32,2048]{3,2,1,0:T(8,128)(2,1)} async-done(((bf16[16,2,32,2048]{3,2,1,0:T(8,128)(2,1)}), bf16[16,2,32,2048]{3,2,1,0:T(8,128)(2,1)}, u32[]{:S(2)}, u32[]{:S(2)}) %all-to-all-start.3) | async-done | bytes 4194336 | tf_op jit(solution)/shard_map/all_to_all | solution.py:191
  540.9 2.9 convolution_bitcast_fusion
  543.8 3.9 fusion.29
  547.7 35.4 %reduce-scatter.5.cloned.1.call-done = f32[128,1024]{1,0:T(8,128)} async-done(((f32[128,2048]{1,0:T(8,128)}), f32[128,1024]{1,0:T(8,128)}) %reduce-scatter.5.cloned.1.call-update) | async-done | bytes 524304 | tf_op jit(solution)/shard_map/reduce_scatter | solution.py:202
  583.2 1.8 fusion.56
  (171 shorter events, 52.1 us)
Async XLA Ops:
  6.5 301.0 %copy-start = (f32[1024,64]{0,1:T(8,128)S(1)}, f32[1024,64]{0,1:T(8,128)}, u32[]{:S(2)}) copy-start(f32[1024,64]{0,1:T(8,128)} %param.28) | copy-start | bytes 786436
  6.5 119.8 %copy-start.34 = (s32[4]{0:T(128)S(1)}, s32[4]{0:T(128)}, u32[]{:S(2)}) copy-start(s32[4]{0:T(128)} %param.17) | copy-start | bytes 52
  6.5 181.1 %copy-start.30 = (s32[2048]{0:T(1024)S(1)}, s32[2048]{0:T(1024)}, u32[]{:S(2)}) copy-start(s32[2048]{0:T(1024)} %param.18) | copy-start | bytes 24580
  6.5 234.8 %all-gather.2.cloned.1.call-start = ((), (), s32[]{:S(2)}) async-start(), calls=%async_computation.6 | async-start | bytes 8912896 | tf_op jit(solution)/shard_map/all_gather | solution.py:49
  18.8 8.8 %collective-permute-start = (bf16[1024,128]{1,0:T(8,128)(2,1)}, bf16[1024,128]{1,0:T(8,128)(2,1)S(1)}, u32[]{:S(2)}, u32[]{:S(2)}) collective-permute-start(bf16[1024,128]{1,0:T(8,128)(2,1)} %param.27), channel_id=1, source_target_pairs={{0,2},{2,4},{4,6},{6,8},{8,10},{10,12},{12,14},{14,16},{16,18},{18... | collective-permute-start | bytes 786440 | tf_op jit(solution)/shard_map/ppermute | solution.py:112
  27.5 198.5 %copy-start.7 = (bf16[1024,128]{1,0:T(8,128)(2,1)}, bf16[1024,128]{1,0:T(8,128)(2,1)S(1)}, u32[]{:S(2)}) copy-start(bf16[1024,128]{1,0:T(8,128)(2,1)S(1)} %collective-permute-done) | copy-start | bytes 786436
  27.5 12.2 %collective-permute-start.1 = (bf16[1024,128]{1,0:T(8,128)(2,1)S(1)}, bf16[1024,128]{1,0:T(8,128)(2,1)S(1)}, u32[]{:S(2)}, u32[]{:S(2)}) collective-permute-start(bf16[1024,128]{1,0:T(8,128)(2,1)S(1)} %collective-permute-done), channel_id=1, source_target_pairs={{0,2},{2,4},{4,6},{6,8},{8,10},{10,12},{12,14},{14,16},{16,18},{18... | collective-permute-start | bytes 786440 | tf_op jit(solution)/shard_map/ppermute | solution.py:112
  39.7 185.6 %copy-start.9 = (bf16[1024,128]{1,0:T(8,128)(2,1)}, bf16[1024,128]{1,0:T(8,128)(2,1)S(1)}, u32[]{:S(2)}) copy-start(bf16[1024,128]{1,0:T(8,128)(2,1)S(1)} %collective-permute-done.1) | copy-start | bytes 786436
  39.7 14.1 %collective-permute-start.2 = (bf16[1024,128]{1,0:T(8,128)(2,1)S(1)}, bf16[1024,128]{1,0:T(8,128)(2,1)S(1)}, u32[]{:S(2)}, u32[]{:S(2)}) collective-permute-start(bf16[1024,128]{1,0:T(8,128)(2,1)S(1)} %collective-permute-done.1), channel_id=1, source_target_pairs={{0,2},{2,4},{4,6},{6,8},{8,10},{10,12},{12,14},{14,16},{16,18},{18... | collective-permute-start | bytes 786440 | tf_op jit(solution)/shard_map/ppermute | solution.py:112
  53.8 170.7 %copy-start.11 = (bf16[1024,128]{1,0:T(8,128)(2,1)}, bf16[1024,128]{1,0:T(8,128)(2,1)S(1)}, u32[]{:S(2)}) copy-start(bf16[1024,128]{1,0:T(8,128)(2,1)S(1)} %collective-permute-done.2) | copy-start | bytes 786436
  53.8 8.6 %collective-permute-start.3 = (bf16[1024,128]{1,0:T(8,128)(2,1)S(1)}, bf16[1024,128]{1,0:T(8,128)(2,1)S(1)}, u32[]{:S(2)}, u32[]{:S(2)}) collective-permute-start(bf16[1024,128]{1,0:T(8,128)(2,1)S(1)} %collective-permute-done.2), channel_id=1, source_target_pairs={{0,2},{2,4},{4,6},{6,8},{8,10},{10,12},{12,14},{14,16},{16,18},{18... | collective-permute-start | bytes 786440 | tf_op jit(solution)/shard_map/ppermute | solution.py:112
  63.1 14.1 %collective-permute-start.4 = (bf16[1024,128]{1,0:T(8,128)(2,1)S(1)}, bf16[1024,128]{1,0:T(8,128)(2,1)S(1)}, u32[]{:S(2)}, u32[]{:S(2)}) collective-permute-start(bf16[1024,128]{1,0:T(8,128)(2,1)S(1)} %collective-permute-done.3), channel_id=1, source_target_pairs={{0,2},{2,4},{4,6},{6,8},{8,10},{10,12},{12,14},{14,16},{16,18},{18... | collective-permute-start | bytes 786440 | tf_op jit(solution)/shard_map/ppermute | solution.py:112
  77.9 14.1 %collective-permute-start.5 = (bf16[1024,128]{1,0:T(8,128)(2,1)S(1)}, bf16[1024,128]{1,0:T(8,128)(2,1)S(1)}, u32[]{:S(2)}, u32[]{:S(2)}) collective-permute-start(bf16[1024,128]{1,0:T(8,128)(2,1)S(1)} %collective-permute-done.4), channel_id=1, source_target_pairs={{0,2},{2,4},{4,6},{6,8},{8,10},{10,12},{12,14},{14,16},{16,18},{18... | collective-permute-start | bytes 786440 | tf_op jit(solution)/shard_map/ppermute | solution.py:112
  92.7 13.3 %collective-permute-start.6 = (bf16[1024,128]{1,0:T(8,128)(2,1)S(1)}, bf16[1024,128]{1,0:T(8,128)(2,1)S(1)}, u32[]{:S(2)}, u32[]{:S(2)}) collective-permute-start(bf16[1024,128]{1,0:T(8,128)(2,1)S(1)} %collective-permute-done.5), channel_id=1, source_target_pairs={{0,2},{2,4},{4,6},{6,8},{8,10},{10,12},{12,14},{14,16},{16,18},{18... | collective-permute-start | bytes 786440 | tf_op jit(solution)/shard_map/ppermute | solution.py:112
  106.7 8.5 %collective-permute-start.7 = (bf16[1024,128]{1,0:T(8,128)(2,1)S(1)}, bf16[1024,128]{1,0:T(8,128)(2,1)S(1)}, u32[]{:S(2)}, u32[]{:S(2)}) collective-permute-start(bf16[1024,128]{1,0:T(8,128)(2,1)S(1)} %collective-permute-done.6), channel_id=1, source_target_pairs={{0,2},{2,4},{4,6},{6,8},{8,10},{10,12},{12,14},{14,16},{16,18},{18... | collective-permute-start | bytes 786440 | tf_op jit(solution)/shard_map/ppermute | solution.py:112
  115.2 80.9 %copy-start.17 = (bf16[1024,128]{1,0:T(8,128)(2,1)}, bf16[1024,128]{1,0:T(8,128)(2,1)S(1)}, u32[]{:S(2)}) copy-start(bf16[1024,128]{1,0:T(8,128)(2,1)S(1)} %collective-permute-done.7) | copy-start | bytes 786436
  115.2 11.3 %collective-permute-start.8 = (bf16[1024,128]{1,0:T(8,128)(2,1)S(1)}, bf16[1024,128]{1,0:T(8,128)(2,1)S(1)}, u32[]{:S(2)}, u32[]{:S(2)}) collective-permute-start(bf16[1024,128]{1,0:T(8,128)(2,1)S(1)} %collective-permute-done.7), channel_id=1, source_target_pairs={{0,2},{2,4},{4,6},{6,8},{8,10},{10,12},{12,14},{14,16},{16,18},{18... | collective-permute-start | bytes 786440 | tf_op jit(solution)/shard_map/ppermute | solution.py:112
  119.2 107.6 %copy-start.4 = (bf16[1024,128]{1,0:T(8,128)(2,1)S(1)}, bf16[1024,128]{1,0:T(8,128)(2,1)}, u32[]{:S(2)}) copy-start(bf16[1024,128]{1,0:T(8,128)(2,1)} %param.27) | copy-start | bytes 786436
  120.6 120.7 %all-to-all-start = ((bf16[16,128,384]{2,1,0:T(8,128)(2,1)}), bf16[16,128,384]{2,1,0:T(8,128)(2,1)}, u32[]{:S(2)}, u32[]{:S(2)}) async-start(bf16[16,128,384]{2,1,0:T(8,128)(2,1)} %bitcast.10), calls=%async_computation | async-start | bytes 3145728 | tf_op jit(solution)/shard_map/all_to_all | solution.py:102
  126.5 69.6 %copy-start.19 = (bf16[1024,128]{1,0:T(8,128)(2,1)}, bf16[1024,128]{1,0:T(8,128)(2,1)S(1)}, u32[]{:S(2)}) copy-start(bf16[1024,128]{1,0:T(8,128)(2,1)S(1)} %collective-permute-done.8) | copy-start | bytes 786436
  126.5 34.0 %collective-permute-start.9 = (bf16[1024,128]{1,0:T(8,128)(2,1)S(1)}, bf16[1024,128]{1,0:T(8,128)(2,1)S(1)}, u32[]{:S(2)}, u32[]{:S(2)}) collective-permute-start(bf16[1024,128]{1,0:T(8,128)(2,1)S(1)} %collective-permute-done.8), channel_id=1, source_target_pairs={{0,2},{2,4},{4,6},{6,8},{8,10},{10,12},{12,14},{14,16},{16,18},{18... | collective-permute-start | bytes 786440 | tf_op jit(solution)/shard_map/ppermute | solution.py:112
  161.2 8.6 %collective-permute-start.10 = (bf16[1024,128]{1,0:T(8,128)(2,1)S(1)}, bf16[1024,128]{1,0:T(8,128)(2,1)S(1)}, u32[]{:S(2)}, u32[]{:S(2)}) collective-permute-start(bf16[1024,128]{1,0:T(8,128)(2,1)S(1)} %collective-permute-done.9), channel_id=1, source_target_pairs={{0,2},{2,4},{4,6},{6,8},{8,10},{10,12},{12,14},{14,16},{16,18},{18... | collective-permute-start | bytes 786440 | tf_op jit(solution)/shard_map/ppermute | solution.py:112
  170.6 8.5 %collective-permute-start.11 = (bf16[1024,128]{1,0:T(8,128)(2,1)S(1)}, bf16[1024,128]{1,0:T(8,128)(2,1)S(1)}, u32[]{:S(2)}, u32[]{:S(2)}) collective-permute-start(bf16[1024,128]{1,0:T(8,128)(2,1)S(1)} %collective-permute-done.10), channel_id=1, source_target_pairs={{0,2},{2,4},{4,6},{6,8},{8,10},{10,12},{12,14},{14,16},{16,18},{18... | collective-permute-start | bytes 786440 | tf_op jit(solution)/shard_map/ppermute | solution.py:112
  179.0 17.1 %copy-start.25 = (bf16[1024,128]{1,0:T(8,128)(2,1)}, bf16[1024,128]{1,0:T(8,128)(2,1)S(1)}, u32[]{:S(2)}) copy-start(bf16[1024,128]{1,0:T(8,128)(2,1)S(1)} %collective-permute-done.11) | copy-start | bytes 786436
  179.0 8.5 %collective-permute-start.12 = (bf16[1024,128]{1,0:T(8,128)(2,1)S(1)}, bf16[1024,128]{1,0:T(8,128)(2,1)S(1)}, u32[]{:S(2)}, u32[]{:S(2)}) collective-permute-start(bf16[1024,128]{1,0:T(8,128)(2,1)S(1)} %collective-permute-done.11), channel_id=1, source_target_pairs={{0,2},{2,4},{4,6},{6,8},{8,10},{10,12},{12,14},{14,16},{16,18},{18... | collective-permute-start | bytes 786440 | tf_op jit(solution)/shard_map/ppermute | solution.py:112
  187.5 8.6 %copy-start.27 = (bf16[1024,128]{1,0:T(8,128)(2,1)}, bf16[1024,128]{1,0:T(8,128)(2,1)S(1)}, u32[]{:S(2)}) copy-start(bf16[1024,128]{1,0:T(8,128)(2,1)S(1)} %collective-permute-done.12) | copy-start | bytes 786436
  187.5 8.6 %collective-permute-start.13 = (bf16[1024,128]{1,0:T(8,128)(2,1)S(1)}, bf16[1024,128]{1,0:T(8,128)(2,1)}, u32[]{:S(2)}, u32[]{:S(2)}) collective-permute-start(bf16[1024,128]{1,0:T(8,128)(2,1)S(1)} %collective-permute-done.12), channel_id=1, source_target_pairs={{0,2},{2,4},{4,6},{6,8},{8,10},{10,12},{12,14},{14,16},{16,18},{18... | collective-permute-start | bytes 786440 | tf_op jit(solution)/shard_map/ppermute | solution.py:112
  187.6 43.9 %copy-start.24 = (bf16[1024,128]{1,0:T(8,128)(2,1)S(1)}, bf16[1024,128]{1,0:T(8,128)(2,1)}, u32[]{:S(2)}) copy-start(bf16[1024,128]{1,0:T(8,128)(2,1)} %copy-done.23) | copy-start | bytes 786436
  187.6 44.6 %copy-start.22 = (bf16[1024,128]{1,0:T(8,128)(2,1)S(1)}, bf16[1024,128]{1,0:T(8,128)(2,1)}, u32[]{:S(2)}) copy-start(bf16[1024,128]{1,0:T(8,128)(2,1)} %copy-done.21) | copy-start | bytes 786436
  196.2 8.8 %collective-permute-start.14 = (bf16[1024,128]{1,0:T(8,128)(2,1)}, bf16[1024,128]{1,0:T(8,128)(2,1)S(1)}, u32[]{:S(2)}, u32[]{:S(2)}) collective-permute-start(bf16[1024,128]{1,0:T(8,128)(2,1)} %collective-permute-done.13), channel_id=1, source_target_pairs={{0,2},{2,4},{4,6},{6,8},{8,10},{10,12},{12,14},{14,16},{16,18},{18... | collective-permute-start | bytes 786440 | tf_op jit(solution)/shard_map/ppermute | solution.py:112
  196.2 33.7 %copy-start.28 = (bf16[1024,128]{1,0:T(8,128)(2,1)S(1)}, bf16[1024,128]{1,0:T(8,128)(2,1)}, u32[]{:S(2)}) copy-start(bf16[1024,128]{1,0:T(8,128)(2,1)} %copy-done.27) | copy-start | bytes 786436
  196.2 34.5 %copy-start.26 = (bf16[1024,128]{1,0:T(8,128)(2,1)S(1)}, bf16[1024,128]{1,0:T(8,128)(2,1)}, u32[]{:S(2)}) copy-start(bf16[1024,128]{1,0:T(8,128)(2,1)} %copy-done.25) | copy-start | bytes 786436
  196.3 36.7 %copy-start.20 = (bf16[1024,128]{1,0:T(8,128)(2,1)S(1)}, bf16[1024,128]{1,0:T(8,128)(2,1)}, u32[]{:S(2)}) copy-start(bf16[1024,128]{1,0:T(8,128)(2,1)} %copy-done.19) | copy-start | bytes 786436
  196.3 37.5 %copy-start.18 = (bf16[1024,128]{1,0:T(8,128)(2,1)S(1)}, bf16[1024,128]{1,0:T(8,128)(2,1)}, u32[]{:S(2)}) copy-start(bf16[1024,128]{1,0:T(8,128)(2,1)} %copy-done.17) | copy-start | bytes 786436
  266.0 9.6 %copy-start.12 = (bf16[1024,128]{1,0:T(8,128)(2,1)S(1)}, bf16[1024,128]{1,0:T(8,128)(2,1)}, u32[]{:S(2)}) copy-start(bf16[1024,128]{1,0:T(8,128)(2,1)} %copy-done.11) | copy-start | bytes 786436
  266.0 10.3 %copy-start.10 = (bf16[1024,128]{1,0:T(8,128)(2,1)S(1)}, bf16[1024,128]{1,0:T(8,128)(2,1)}, u32[]{:S(2)}) copy-start(bf16[1024,128]{1,0:T(8,128)(2,1)} %copy-done.9) | copy-start | bytes 786436
  266.0 11.1 %copy-start.8 = (bf16[1024,128]{1,0:T(8,128)(2,1)S(1)}, bf16[1024,128]{1,0:T(8,128)(2,1)}, u32[]{:S(2)}) copy-start(bf16[1024,128]{1,0:T(8,128)(2,1)} %copy-done.7) | copy-start | bytes 786436
  266.0 11.9 %copy-start.5 = (bf16[1024,128]{1,0:T(8,128)(2,1)S(1)}, bf16[1024,128]{1,0:T(8,128)(2,1)}, u32[]{:S(2)}) copy-start(bf16[1024,128]{1,0:T(8,128)(2,1)} %param.27) | copy-start | bytes 786436
  271.2 16.5 %copy-start.31 = (s32[128,8]{0,1:T(8,128)S(1)}, s32[128,8]{0,1:T(8,128)}, u32[]{:S(2)}) copy-start(s32[128,8]{0,1:T(8,128)} %param.19) | copy-start | bytes 12292
  271.2 35.1 %copy-start.6 = (bf16[128,1024]{1,0:T(8,128)(2,1)S(1)}, bf16[128,1024]{1,0:T(8,128)(2,1)}, u32[]{:S(2)}) copy-start(bf16[128,1024]{1,0:T(8,128)(2,1)} %param.16) | copy-start | bytes 786436
  271.2 36.3 %copy-start.29 = (f32[1024]{0:T(1024)S(1)}, f32[1024]{0:T(1024)}, u32[]{:S(2)}) copy-start(f32[1024]{0:T(1024)} %param.21) | copy-start | bytes 12292
  272.1 11.6 %all-to-all-start.1 = ((bf16[8,128,128]{1,2,0:T(8,128)(2,1)}), bf16[8,128,128]{1,2,0:T(8,128)(2,1)S(1)}, u32[]{:S(2)}, u32[]{:S(2)}) async-start(bf16[8,128,128]{1,2,0:T(8,128)(2,1)} %copy.45), calls=%async_computation.1 | async-start | bytes 524288 | tf_op jit(solution)/shard_map/all_to_all | solution.py:133
  275.5 30.8 %reduce-scatter.3.cloned.1.call-start = ((), (), s32[]{:S(2)}) async-start(), calls=%async_computation.7 | async-start | bytes 1572864 | tf_op jit(solution)/shard_map/reduce_scatter | solution.py:143
  323.9 98.8 %slice-start = ((s8[8388608]{0:T(1024)(128)(4,1)}), s8[4194304]{0:T(1024)(128)(4,1)S(1)}, s32[]{:S(2)}) async-start(s8[8388608]{0:T(1024)(128)(4,1)} %bitcast.118), calls=%async_computation.9 | async-start | bytes 8388608
  422.7 10.0 %copy-start.3 = (bf16[16,1,32,2048]{3,2,1,0:T(8,128)(2,1)}, bf16[16,1,32,2048]{3,2,1,0:T(8,128)(2,1)S(1)}, u32[]{:S(2)}) copy-start(bf16[16,1,32,2048]{3,2,1,0:T(8,128)(2,1)S(1)} %get-tuple-element.10) | copy-start | bytes 6291460
  457.8 83.0 %all-to-all-start.3 = ((bf16[16,2,32,2048]{3,2,1,0:T(8,128)(2,1)}), bf16[16,2,32,2048]{3,2,1,0:T(8,128)(2,1)}, u32[]{:S(2)}, u32[]{:S(2)}) async-start(bf16[16,2,32,2048]{3,2,1,0:T(8,128)(2,1)} %pad_maximum_fusion), calls=%async_computation.4 | async-start | bytes 8388608 | tf_op jit(solution)/shard_map/all_to_all | solution.py:191
  463.2 120.0 %reduce-scatter.5.cloned.1.call-start = ((), (), s32[]{:S(2)}) async-start(), calls=%async_computation.8 | async-start | bytes 1572864 | tf_op jit(solution)/shard_map/reduce_scatter | solution.py:202
  463.3 121.7 %copy-start.1 = (f32[1024,64]{0,1:T(8,128)S(1)}, f32[1024,64]{0,1:T(8,128)}, u32[]{:S(2)}) copy-start(f32[1024,64]{0,1:T(8,128)} %param.28) | copy-start | bytes 786436
  (10 other events, 22.3 us)
Sparse Core Ops, SparseCore 0:
  18.9 86.8 all-gather.1
  287.7 18.5 reduce-scatter.2
  547.9 35.2 reduce-scatter.4
